TPU v7x, 256 devices: a whole 4x4x8 slice. The times are simulated.
256 devices in a mesh: grid: 64 (over z, y, core), lev: 4 (over x).
Axes of the slice: x: 4, y: 4, z: 8, core: 2. Of those that a mesh axis runs over, the one named last changes fastest.
Arguments:
- prior_fields: float32 [128, 8, 32768], P('grid', 'lev'), may hold values from -6 to 6
- channel_weights: float32 [8, 4], P('lev'), may hold values from 0.1 to 1
- obs_owner: int32 [4], replicated, may hold values from 0 to 63
- obs_offset: int32 [4, 4, 64], replicated, may hold values from 0 to 511
- obs_value: float32 [4, 4, 64], P(None, 'lev'), may hold values from -30 to 30
- obs_error: float32 [4, 4, 64], P(None, 'lev'), may hold values from 0.5 to 2
- ancestors: int32 [4, 4, 64, 128], P(None, 'lev', 'grid'), may hold values from 0 to 127
Outputs:
- posterior_fields: float32 [128, 8, 32768], P('grid', 'lev')
All inputs are finite; a program needn't handle non-finite values.
Results may differ from a plain program's by a relative error of at most 0.0003.
Values sent between devices are 32-bit elements; how exact they have to be, the bound alone decides.
A program may use at most 128 MiB of HBM per device.

v0:
```python
import jax
import jax.numpy as jnp
from jax import lax
from jax.sharding import PartitionSpec as P

NB = 4


HIGH = lax.Precision.HIGHEST


def spread(value, axis, source):
    kept = jnp.where(lax.axis_index(axis) == source, value, 0).astype(value.dtype)
    return lax.psum(kept, axis)


def blend_matrices(prior_obs, observed, obs_dev, centres, positions, scale, parents):
    count = observed.shape[0]
    members = prior_obs.shape[1]
    innovation = ((observed[:, None] - prior_obs) / obs_dev[:, None]) ** 2
    distance = (centres[:, None] - positions[None, :]) / scale
    taper = jnp.exp(-0.5 * distance * distance)
    log_weight = -0.5 / count * jnp.dot(taper, innovation, precision=HIGH)
    top_value = jnp.max(log_weight, axis=1, keepdims=True)
    expo_weight = jnp.exp(log_weight - top_value)
    weight = expo_weight / jnp.sum(expo_weight, axis=1, keepdims=True)
    alpha = 0.8 * (1.0 - jnp.exp(-jnp.sum(taper, axis=1) / count))
    onehot = (parents[:, :, None] == jnp.arange(members, dtype=jnp.int32)[None, None, :]).astype(
        jnp.float32
    )
    identity = jnp.eye(members, dtype=jnp.float32)
    remain = 1.0 - alpha
    return (
        alpha[:, None, None] * onehot
        + remain[:, None, None] * identity[None]
        + (weight - 1.0 / members)[:, None, :]
    )


def body(prior_fields, channel_weights, obs_owner, obs_offset, obs_value, obs_error, ancestors):
    grid_count = lax.axis_size("grid")
    member_slab, group_depth, cells = prior_fields.shape
    members = member_slab * grid_count
    block_cells = cells // grid_count
    local_regions = ancestors.shape[2]
    region_cells = block_cells // local_regions
    scale = local_regions * grid_count / 2.0
    groups = channel_weights.shape[1]
    count = obs_offset.shape[2]
    group = lax.axis_index("lev")
    block = lax.axis_index("grid")
    region_list = jnp.arange(local_regions, dtype=jnp.int32)
    centres = (block * local_regions + region_list).astype(jnp.float32) + 0.5
    first_cells = obs_offset[0].reshape(-1)
    fields = lax.all_to_all(prior_fields, "grid", split_axis=2, concat_axis=0, tiled=True)
    picked = fields[:, :, first_cells]
    for batch in range(NB):
        owner = obs_owner[batch]
        if batch > 0:
            picked = fields[:, :, obs_offset[batch].reshape(-1)]
        partial_value = jnp.einsum(
            "mlgk,lg->gkm",
            picked.reshape(members, group_depth, groups, count),
            channel_weights,
            precision=HIGH,
        )
        shared = spread(partial_value, "grid", owner)
        priors = lax.psum(shared, "lev")
        own_priors = lax.dynamic_index_in_dim(priors, group, 0, keepdims=False)
        own_offsets = lax.dynamic_index_in_dim(obs_offset[batch], group, 0, keepdims=False)
        positions = (owner * block_cells + own_offsets).astype(jnp.float32) / region_cells
        blend = blend_matrices(
            own_priors,
            obs_value[batch, 0],
            obs_error[batch, 0],
            centres,
            positions,
            scale,
            ancestors[batch, 0],
        )
        slab = fields.reshape(members, group_depth, local_regions, region_cells)
        mixed = jnp.einsum("rjm,mlrc->jlrc", blend, slab, precision=HIGH)
        fields = mixed.reshape(members, group_depth, block_cells)
    return lax.all_to_all(fields, "grid", split_axis=0, concat_axis=2, tiled=True)


def solution(mesh):
    in_specs = (
        P("grid", "lev", None),
        P("lev", None),
        P(),
        P(),
        P(None, "lev", None),
        P(None, "lev", None),
        P(None, "lev", "grid", None),
    )
    out_specs = P("grid", "lev", None)
    return jax.shard_map(body, mesh=mesh, in_specs=in_specs, out_specs=out_specs, check_vma=False)
```

profile of v0, /device:TPU:1, one launch (start us, length us, event | category | flops | bytes accessed | tf_op | source)
XLA Modules:
  0.0 1151.4 jit_solution(4428390036950253252)
XLA Ops:
  6.5 32.4 %copy.30 = f32[2,2,32768]{1,0,2:T(2,128)} copy(f32[2,2,32768]{2,1,0:T(2,128)} %param.7) | data formatting | bytes 1048576 | tf_op args[0]
  39.0 49.5 %reshape.797 = f32[64,1,2048]{2,1,0:T(1,128)} reshape(f32[32768,2,2]{2,1,0:T(2,128)} %bitcast.174) | data formatting | bytes 1048576
  88.5 13.2 %all-to-all-start = ((f32[64,1,2048]{2,1,0:T(1,128)}), f32[64,1,2048]{2,1,0:T(1,128)S(1)}, u32[]{:S(2)}, u32[]{:S(2)}) async-start(f32[64,1,2048]{2,1,0:T(1,128)} %reshape.797), calls=%async_computation | async-start | bytes 1048576 | tf_op jit(solution)/shard_map/all_to_all | solution.py:55
  101.9 0.7 fusion.106
  103.3 16.1 %all-to-all-done = f32[64,1,2048]{2,1,0:T(1,128)S(1)} async-done(((f32[64,1,2048]{2,1,0:T(1,128)}), f32[64,1,2048]{2,1,0:T(1,128)S(1)}, u32[]{:S(2)}, u32[]{:S(2)}) %all-to-all-start) | async-done | bytes 524320 | tf_op jit(solution)/shard_map/all_to_all | solution.py:55
  119.4 0.5 broadcast.610
  119.9 1.9 reduce.32
  121.8 53.4 %reshape.798 = f32[32768,2,2]{2,1,0:T(2,128)} reshape(f32[64,2048]{1,0:T(8,128)S(1)} %reduce.32) | data formatting | bytes 1048576
  175.2 35.6 %copy.31 = f32[2,2,64,512]{3,0,2,1:T(2,128)S(1)} copy(f32[2,2,64,512]{1,0,3,2:T(2,128)} %bitcast.173) | data formatting | bytes 1048576 | tf_op jit(solution)/shard_map/all_to_all | solution.py:55
  211.5 1.0 gather_fusion
  212.6 0.7 select_bitcast_fusion.3
  214.0 169.1 %all-reduce.9.cloned.1.call-done = f32[4,64,128]{2,1,0:T(8,128)} async-done(((f32[4,64,128]{2,1,0:T(8,128)}), f32[4,64,128]{2,1,0:T(8,128)}) %all-reduce.9.cloned.1.call-update) | async-done | bytes 131088 | tf_op jit(solution)/shard_map/psum | solution.py:14
  383.2 0.6 fusion.104
  385.4 41.5 %all-reduce.11.cloned.1.call-done = f32[4,64,128]{2,1,0:T(8,128)} async-done(((f32[4,64,128]{2,1,0:T(8,128)}), f32[4,64,128]{2,1,0:T(8,128)}) %all-reduce.11.cloned.1.call-update) | async-done | bytes 131088 | tf_op jit(solution)/shard_map/psum | solution.py:68
  426.9 1.6 fusion.107
  428.4 1.3 fusion.97
  429.8 1.3 divide_add_fusion.3
  431.1 0.6 fusion.7
  432.0 1.0 gather_fusion.1
  433.1 0.7 select_bitcast_fusion.2
  434.5 175.3 %all-reduce.13.cloned.1.call-done = f32[4,64,128]{2,1,0:T(8,128)} async-done(((f32[4,64,128]{2,1,0:T(8,128)}), f32[4,64,128]{2,1,0:T(8,128)}) %all-reduce.13.cloned.1.call-update) | async-done | bytes 131088 | tf_op jit(solution)/shard_map/psum | solution.py:14
  610.1 0.6 fusion.103
  612.1 41.4 %all-reduce.15.cloned.1.call-done = f32[4,64,128]{2,1,0:T(8,128)} async-done(((f32[4,64,128]{2,1,0:T(8,128)}), f32[4,64,128]{2,1,0:T(8,128)}) %all-reduce.15.cloned.1.call-update) | async-done | bytes 131088 | tf_op jit(solution)/shard_map/psum | solution.py:68
  653.5 1.6 fusion.108
  655.1 1.3 fusion.98
  656.4 1.3 divide_add_fusion.2
  657.8 1.0 convolution_bitcast_fusion.2
  658.8 0.4 copy.37
  659.2 1.0 gather_fusion.2
  660.6 0.7 select_bitcast_fusion.1
  662.0 175.4 %all-reduce.17.cloned.1.call-done = f32[4,64,128]{2,1,0:T(8,128)} async-done(((f32[4,64,128]{2,1,0:T(8,128)}), f32[4,64,128]{2,1,0:T(8,128)}) %all-reduce.17.cloned.1.call-update) | async-done | bytes 131088 | tf_op jit(solution)/shard_map/psum | solution.py:14
  837.4 0.6 fusion.102
  839.4 41.5 %all-reduce.19.cloned.1.call-done = f32[4,64,128]{2,1,0:T(8,128)} async-done(((f32[4,64,128]{2,1,0:T(8,128)}), f32[4,64,128]{2,1,0:T(8,128)}) %all-reduce.19.cloned.1.call-update) | async-done | bytes 131088 | tf_op jit(solution)/shard_map/psum | solution.py:68
  880.9 1.6 fusion.109
  882.5 1.3 fusion.99
  883.9 1.3 divide_add_fusion.1
  885.2 0.7 convolution_bitcast_fusion.1
  886.3 1.0 gather_fusion.3
  887.7 0.7 select_bitcast_fusion
  888.4 176.1 %all-reduce.21.cloned.1.call-done = f32[4,64,128]{2,1,0:T(8,128)} async-done(((f32[4,64,128]{2,1,0:T(8,128)}), f32[4,64,128]{2,1,0:T(8,128)}) %all-reduce.21.cloned.1.call-update) | async-done | bytes 131088 | tf_op jit(solution)/shard_map/psum | solution.py:14
  1065.2 0.6 fusion.101
  1066.5 41.8 %all-reduce.23.cloned.1.call-done = f32[4,64,128]{2,1,0:T(8,128)} async-done(((f32[4,64,128]{2,1,0:T(8,128)}), f32[4,64,128]{2,1,0:T(8,128)}) %all-reduce.23.cloned.1.call-update) | async-done | bytes 131088 | tf_op jit(solution)/shard_map/psum | solution.py:68
  1108.3 1.6 fusion.110
  1109.9 1.3 fusion.100
  1111.2 1.3 divide_add_fusion
  1112.6 0.7 convolution_bitcast_fusion
  1113.5 30.3 %all_to_all.36 = f32[128,2,512]{2,1,0:T(2,128)S(1)} all-to-all(f32[128,2,512]{2,1,0:T(2,128)S(1)} %copy.39), channel_id=1, replica_groups=mesh['grid'=64,'lev'=4] {'grid'}, dimensions={0} | all-to-all | bytes 1048576 | tf_op jit(solution)/shard_map/all_to_all | solution.py:84
  1143.7 0.8 copy.67
  (53 shorter events, 3.6 us)
Async XLA Ops:
  39.0 62.8 %copy-start.1 = (s32[4,4,64]{2,1,0:T(4,128)S(1)}, s32[4,4,64]{2,1,0:T(4,128)}, u32[]{:S(2)}) copy-start(s32[4,4,64]{2,1,0:T(4,128)} %param.10) | copy-start | bytes 12292
  39.0 63.0 %copy-start.2 = (s32[4]{0:T(128)S(1)}, s32[4]{0:T(128)}, u32[]{:S(2)}) copy-start(s32[4]{0:T(128)} %param.9) | copy-start | bytes 52
  39.0 64.3 %copy-start.4 = (f32[4,1,64]{2,1,0:T(1,128)S(1)}, f32[4,1,64]{2,1,0:T(1,128)}, u32[]{:S(2)}) copy-start(f32[4,1,64]{2,1,0:T(1,128)} %param.12) | copy-start | bytes 3076
  39.0 64.3 %copy-start.5 = (f32[4,1,64]{2,1,0:T(1,128)S(1)}, f32[4,1,64]{2,1,0:T(1,128)}, u32[]{:S(2)}) copy-start(f32[4,1,64]{2,1,0:T(1,128)} %param.11) | copy-start | bytes 3076
  88.5 30.9 %all-to-all-start = ((f32[64,1,2048]{2,1,0:T(1,128)}), f32[64,1,2048]{2,1,0:T(1,128)S(1)}, u32[]{:S(2)}, u32[]{:S(2)}) async-start(f32[64,1,2048]{2,1,0:T(1,128)} %reshape.797), calls=%async_computation | async-start | bytes 1048576 | tf_op jit(solution)/shard_map/all_to_all | solution.py:55
  101.7 281.4 %all-reduce.9.cloned.1.call-start = ((), (), s32[]{:S(2)}) async-start(), calls=%async_computation.2 | async-start | bytes 262144 | tf_op jit(solution)/shard_map/psum | solution.py:14
  175.2 37.3 %copy-start = (f32[2,4]{1,0:T(2,128)S(1)}, f32[2,4]{1,0:T(2,128)}, u32[]{:S(2)}) copy-start(f32[2,4]{1,0:T(2,128)} %param.8) | copy-start | bytes 100
  175.2 38.1 %copy-start.3 = (s32[4,1,1,128]{3,2,1,0:T(1,128)S(1)}, s32[4,1,1,128]{3,2,1,0:T(1,128)}, u32[]{:S(2)}) copy-start(s32[4,1,1,128]{3,2,1,0:T(1,128)} %param.13) | copy-start | bytes 6148
  213.3 213.6 %all-reduce.11.cloned.1.call-start = ((), (), s32[]{:S(2)}) async-start(), calls=%async_computation.3 | async-start | bytes 262144 | tf_op jit(solution)/shard_map/psum | solution.py:68
  383.1 226.7 %all-reduce.13.cloned.1.call-start = ((), (), s32[]{:S(2)}) async-start(), calls=%async_computation.4 | async-start | bytes 262144 | tf_op jit(solution)/shard_map/psum | solution.py:14
  433.8 219.7 %all-reduce.15.cloned.1.call-start = ((), (), s32[]{:S(2)}) async-start(), calls=%async_computation.5 | async-start | bytes 262144 | tf_op jit(solution)/shard_map/psum | solution.py:68
  609.8 227.5 %all-reduce.17.cloned.1.call-start = ((), (), s32[]{:S(2)}) async-start(), calls=%async_computation.6 | async-start | bytes 262144 | tf_op jit(solution)/shard_map/psum | solution.py:14
  661.3 219.6 %all-reduce.19.cloned.1.call-start = ((), (), s32[]{:S(2)}) async-start(), calls=%async_computation.7 | async-start | bytes 262144 | tf_op jit(solution)/shard_map/psum | solution.py:68
  837.4 227.1 %all-reduce.21.cloned.1.call-start = ((), (), s32[]{:S(2)}) async-start(), calls=%async_computation.8 | async-start | bytes 262144 | tf_op jit(solution)/shard_map/psum | solution.py:14
  888.3 220.0 %all-reduce.23.cloned.1.call-start = ((), (), s32[]{:S(2)}) async-start(), calls=%async_computation.9 | async-start | bytes 262144 | tf_op jit(solution)/shard_map/psum | solution.py:68
Sparse Core Ops, SparseCore 0:
  213.4 169.6 all-reduce.8
  385.4 41.3 all-reduce.10
  433.9 175.8 all-reduce.12
  612.1 41.3 all-reduce.14
  661.4 175.8 all-reduce.16
  839.5 41.3 all-reduce.18
  888.5 175.9 all-reduce.20
  1066.9 41.3 all-reduce.22
where the time goes:
time: 1160 us; the launch traced here: 1150 us
  waiting for transfers between devices  878 us (76%)
  local copies, waits for them, and re-layouts  179 us (15%)
  blocking collectives  30.3 us (3%)
  between operations  21.8 us (2%)
  other arithmetic  18.7 us (2%)
  starting transfers between devices  13.7 us (1%)
    psum x4, waiting for transfers between devices, spread(): return lax.psum(kept, axis)  696 us
    psum x4, waiting for transfers between devices, body(): priors = lax.psum(shared, 'lev')  166 us
    unnamed x18, local copies, waits for them, and re-layouts  136 us
    all_to_all x4, local copies, waits for them, and re-layouts, body(): lax.all_to_all(prior_fields, 'grid', split_axis=2, concat_axis=0, tiled=T...  36.7 us
    all_to_all x1, blocking collectives, body(): lax.all_to_all(fields, 'grid', split_axis=0, concat_axis=2, tiled=True)  30.3 us
  transfers between devices with their start and end apart: 9, of which 9 were waited for; matrix products, arithmetic and copies ran while one was open for 0% of the time, Pallas kernels for 0%

commit v1 on v0

v1 whole, which is shorter than its diff:
```python
import functools

import jax
import jax.numpy as jnp
from jax import lax
from jax.experimental import pallas as pl
from jax.experimental.pallas import tpu as pltpu
from jax.sharding import PartitionSpec as P

NB = 4
LANES = 128
F32 = jnp.float32
BF16 = jnp.bfloat16
MESH = pl.DeviceIdType.MESH
PAIRS = [(1, 0), (2, 0), (2, 1), (3, 0), (3, 1), (3, 2)]


def iota(shape, axis):
    return lax.broadcasted_iota(jnp.int32, shape, axis)


def split3(v):
    hi = v.astype(BF16)
    rest = v - hi.astype(F32)
    mid = rest.astype(BF16)
    low = (rest - mid.astype(F32)).astype(BF16)
    return hi, mid, low


def dot(a, b):
    return jnp.dot(a, b, preferred_element_type=F32)


def pick_dot(onehot, v):
    hi, mid, low = split3(v)
    return (dot(onehot, low) + dot(onehot, mid)) + dot(onehot, hi)


def kernel(
    n_grid, n_lev, owner, cw, x, off, val, err, anc, out,
    pay, gath, f, y, ys, ssend, srecv, csend, crecv,
    z_sem, y_sem, c_sem, in_sem, out_sem, s_sem, r_sem,
):
    slab = x.shape[0]
    rows = x.shape[1] // n_grid
    members = slab * n_grid
    count = off.shape[2]
    block = rows * LANES // 2
    n_core, n_y = 2, 4
    n_z = n_grid // (n_core * n_y)
    scale = n_grid / 2.0
    per = 12
    prow = per * slab

    me = lax.axis_index("grid")
    lev = lax.axis_index("lev")
    core = me % n_core
    yy = (me // n_core) % n_y
    zz = me // (n_core * n_y)

    def slot_of(g):
        return (g % n_core) * (n_y * n_z) + ((g // n_core) % n_y) * n_z + g // (n_core * n_y)

    def grid_of(s):
        return ((s % n_z) * n_y + (s // n_z) % n_y) * n_core + s // (n_z * n_y)

    my_slot = slot_of(me)

    def send(src, dst, sem, grid, level):
        pltpu.make_async_remote_copy(
            src_ref=src, dst_ref=dst, send_sem=sem.at[0], recv_sem=sem.at[1],
            device_id=(grid, level), device_id_type=MESH,
        ).start()

    def drain(ref, sem):
        pltpu.make_async_copy(ref, ref, sem).wait()

    lane256 = iota((1, n_lev * count), 1)
    wrow = []
    for level in range(2):
        w = jnp.zeros((1, n_lev * count), F32)
        for g in range(n_lev):
            w = jnp.where(lane256 // count == g, cw[level, g], w)
        wrow.append(w)
    row16 = iota((slab * rows, n_lev * count), 0)
    weights = jnp.where(row16 % 2 == 0, wrow[0], wrow[1])
    tile_of_row = (row16 % rows) // 2
    pay[...] = jnp.zeros_like(pay)

    def scan_blocks(k, tiles):
        tile = x[:, pl.ds(pl.multiple_of(k * rows, rows), rows), :]
        return tuple(jnp.where(owner[b] == k, tile, kept) for b, kept in enumerate(tiles))

    zero = jnp.zeros((slab, rows, LANES), F32)
    tiles = lax.fori_loop(0, n_grid, scan_blocks, (zero,) * NB, unroll=8)
    for b in range(NB):
        src = tiles[b].reshape(slab * rows, LANES)
        cells = jnp.concatenate([off[b, g : g + 1, :] for g in range(n_lev)], axis=1)
        onehot = (iota((LANES, n_lev * count), 0) == cells % LANES).astype(BF16)
        hi, mid, low = split3(src)
        got = (dot(low, onehot) + dot(mid, onehot)) + dot(hi, onehot)
        got = jnp.where(tile_of_row == cells // LANES, got * weights, 0.0)
        for i in range(slab):
            value = jnp.sum(got[i * rows : (i + 1) * rows], axis=0, keepdims=True)
            for h in range(2):
                pay[i * per + b * 2 + h : i * per + b * 2 + h + 1, :] = value[:, h * LANES : (h + 1) * LANES]
        pay[2 * NB + b : 2 * NB + b + 1, :] = anc[b].astype(F32)

    my_rows = gath.at[pl.ds(pl.multiple_of(my_slot * prow, 8), prow), :]
    for d in range(1, n_z):
        peer = (((zz + d) % n_z) * n_y + yy) * n_core + core
        send(pay, my_rows, z_sem, peer, lev)
    gath[pl.ds(pl.multiple_of(my_slot * prow, 8), prow), :] = pay[...]

    def push_in(t, carry):
        peer = (me + t) % n_grid
        send(
            x.at[:, pl.ds(pl.multiple_of(peer * rows, rows), rows), :],
            f.at[pl.ds(my_slot * slab, slab)],
            in_sem, peer, lev,
        )
        return carry

    lax.fori_loop(1, n_grid, push_in, 0)
    f[pl.ds(my_slot * slab, slab)] = x[:, pl.ds(pl.multiple_of(me * rows, rows), rows), :]

    drain(gath.at[pl.ds(0, (n_z - 1) * prow), :], z_sem.at[1])
    col_rows = gath.at[pl.ds(pl.multiple_of((core * n_y + yy) * n_z * prow, 8), n_z * prow), :]
    for d in range(1, n_y):
        peer = (zz * n_y + (yy + d) % n_y) * n_core + core
        send(col_rows, col_rows, y_sem, peer, lev)

    lane1 = iota((1, LANES), 1)
    member_row = iota((members, LANES), 0)
    member_lane = iota((members, members), 1)
    eye = (iota((members, members), 0) == member_lane).astype(F32)

    taper = {}
    alpha = {}
    for b in range(NB):
        cells = off[b, pl.ds(lev, 1), :]
        where = (owner[b] * block + cells).astype(F32) / block
        where = jnp.concatenate([where, where], axis=1)
        regions = {0: me}
        for later in range(b + 1, NB):
            regions[later] = owner[later]
        for key, region in regions.items():
            distance = ((region.astype(F32) + 0.5) - where) / scale
            t = jnp.exp(-0.5 * distance * distance)
            taper[b, key] = t
            total = jnp.sum(t, axis=1, keepdims=True)
            alpha[b, key] = 0.8 * (1.0 - jnp.exp(-total / (2 * count)))

    perm = (grid_of(iota((members, members), 0) // slab) * slab + iota((members, members), 0) % slab == member_lane).astype(BF16)

    def columns(stack):
        stack = stack.astype(jnp.int32)
        stack = (slot_of(stack // slab) * slab + stack % slab).astype(F32).astype(BF16)
        return lax.dot_general(perm, stack, (((1,), (1,)), ((), ())), preferred_element_type=F32)

    def picker(cols, k):
        return (cols[:, k : k + 1].astype(jnp.int32) == member_lane).astype(BF16)

    own_cols = columns(pay[8:16, :])
    chain = [eye]
    for b in range(NB):
        a = alpha[b, 0]
        chosen = picker(own_cols, b)
        moved = chosen.astype(F32) if b == 0 else pick_dot(chosen, chain[b])
        chain.append(a * moved + (1.0 - a) * chain[b])

    drain(gath.at[pl.ds(0, (n_y - 1) * n_z * prow), :], y_sem.at[1])
    half = n_y * n_z * prow
    core_rows = gath.at[pl.ds(pl.multiple_of(core * half, 8), half), :]
    send(core_rows, core_rows, c_sem, me + 1 - 2 * core, lev)
    drain(gath.at[pl.ds(0, half), :], c_sem.at[1])

    low_half = iota((members // 2, LANES), 1) < count
    slot_row = iota((n_grid, LANES), 0)
    all_parents = [gath[pl.ds(2 * NB + i, n_grid, stride=prow), :] for i in range(NB - 1)]
    found = [
        jnp.sum(jnp.where(slot_row == slot_of(owner[b]), all_parents[i], 0.0), axis=0, keepdims=True)
        for b, i in PAIRS
    ]
    pair_cols = columns(jnp.concatenate(found + found[:2], axis=0))

    def exchange_base(b, v):
        top, bottom = v[: members // 2], v[members // 2 :]
        for g in range(n_lev):
            lanes = slice((g // 2) * LANES, (g // 2 + 1) * LANES)
            a, c = top[:, lanes], bottom[:, lanes]
            if g % 2 == 0:
                packed = jnp.where(low_half, a, pltpu.roll(c, count, 1))
            else:
                packed = jnp.where(low_half, pltpu.roll(a, count, 1), c)
            ssend[b, g] = packed
        for d in range(1, n_lev):
            level = (lev + d) % n_lev
            send(ssend.at[b, level], srecv.at[b, d - 1], s_sem.at[b], me, level)

    for b in range(NB):
        parts = [gath[pl.ds(b * 2 + h, members, stride=per), :] for h in range(2)]
        v = jnp.concatenate(parts, axis=1)
        for i in range(b):
            ys[PAIRS.index((b, i))] = v
            a = alpha[i, b]
            v = a * pick_dot(picker(pair_cols, PAIRS.index((b, i))), v) + (1.0 - a) * v
        exchange_base(b, v)

    shift = {b: jnp.zeros((1, n_lev * count), F32) for b in range(1, NB)}
    mean_row = jnp.zeros((1, members), F32)
    for b in range(NB):
        drain(srecv.at[b], s_sem.at[b, 1])
        prior = ssend[b, lev]
        for d in range(n_lev - 1):
            prior = prior + srecv[b, d]
        if b > 0:
            for g in range(n_lev):
                row = shift[b][:, (g // 2) * LANES : (g // 2 + 1) * LANES]
                other = pltpu.roll(row, count, 1)
                first = lane1 < count
                row = jnp.where(first, row, other) if g % 2 == 0 else jnp.where(first, other, row)
                csend[b - 1, g] = jnp.broadcast_to(row, (8, LANES))
            for d in range(1, n_lev):
                level = (lev + d) % n_lev
                send(csend.at[b - 1, level], crecv.at[b - 1, d - 1], r_sem.at[b - 1], me, level)
            drain(crecv.at[b - 1], r_sem.at[b - 1, 1])
            row = csend[b - 1, lev]
            for d in range(n_lev - 1):
                row = row + crecv[b - 1, d]
            prior = prior + row[0:1, :]
        seen = jnp.concatenate([val[b], val[b]], axis=1)
        dev = jnp.concatenate([err[b], err[b]], axis=1)
        innovation = ((seen - prior) / dev) ** 2
        for key in [0] + list(range(b + 1, NB)):
            weighted = innovation * taper[b, key]
            top = jnp.sum(jnp.where(low_half, weighted, 0.0), axis=1, keepdims=True)
            bottom = jnp.sum(jnp.where(low_half, 0.0, weighted), axis=1, keepdims=True)
            log_weight = (-0.5 / count) * jnp.concatenate([top, bottom], axis=0)
            expo = jnp.exp(log_weight - jnp.max(log_weight, axis=0, keepdims=True))
            change = expo / jnp.sum(expo, axis=0, keepdims=True) - 1.0 / members
            if key == 0:
                mean_row = mean_row + jnp.sum(change * chain[b], axis=0, keepdims=True)
            else:
                shift[key] = shift[key] + jnp.sum(change * ys[PAIRS.index((key, b))], axis=0, keepdims=True)

    total = chain[NB] + mean_row
    t_hi, t_mid, t_low = split3(total)
    drain(f.at[pl.ds(0, members - slab)], in_sem.at[1])
    f2 = f.reshape(members * rows, LANES)
    y2 = y.reshape(members * rows, LANES)
    for s in range(rows):
        hi, mid, low = split3(f2[pl.ds(s, members, stride=rows), :])
        mixed = (dot(t_low, hi) + dot(t_mid, mid)) + dot(t_hi, low)
        mixed = mixed + (dot(t_mid, hi) + dot(t_hi, mid))
        y2[pl.ds(s, members, stride=rows), :] = mixed + dot(t_hi, hi)

    def push_out(t, carry):
        peer = (me + t) % n_grid
        send(
            y.at[pl.ds(slot_of(peer) * slab, slab)],
            out.at[:, pl.ds(pl.multiple_of(me * rows, rows), rows), :],
            out_sem, peer, lev,
        )
        return carry

    lax.fori_loop(1, n_grid, push_out, 0)
    out[:, pl.ds(pl.multiple_of(me * rows, rows), rows), :] = y[pl.ds(my_slot * slab, slab)]
    drain(y.at[pl.ds(0, members - slab)], out_sem.at[1])

    drain(gath.at[pl.ds(0, (n_z - 1) * prow), :], z_sem.at[0])
    drain(gath.at[pl.ds(0, (n_y - 1) * n_z * prow), :], y_sem.at[0])
    drain(gath.at[pl.ds(0, half), :], c_sem.at[0])
    drain(f.at[pl.ds(0, members - slab)], in_sem.at[0])
    drain(y.at[pl.ds(0, members - slab)], out_sem.at[0])
    for b in range(NB):
        drain(srecv.at[b], s_sem.at[b, 0])
    for b in range(NB - 1):
        drain(crecv.at[b], r_sem.at[b, 0])


def body(n_grid, n_lev, prior_fields, channel_weights, obs_owner, obs_offset, obs_value, obs_error, ancestors):
    slab, depth, cells = prior_fields.shape
    tiles = cells // LANES
    x = prior_fields.reshape(slab, depth, tiles, LANES).transpose(0, 2, 1, 3).reshape(slab, tiles * depth, LANES)
    members = slab * n_grid
    rows = tiles * depth // n_grid
    count = obs_offset.shape[2]
    vm = pl.BlockSpec(memory_space=pltpu.VMEM)
    sm = pl.BlockSpec(memory_space=pltpu.SMEM)
    pair = pltpu.SemaphoreType.DMA((2,))
    out = pl.pallas_call(
        functools.partial(kernel, n_grid, n_lev),
        out_shape=jax.ShapeDtypeStruct((slab, tiles * depth, LANES), F32),
        in_specs=[sm, sm, vm, vm, vm, vm, vm],
        out_specs=vm,
        scratch_shapes=[
            pltpu.VMEM((24, LANES), F32),
            pltpu.VMEM((24 * n_grid, LANES), F32),
            pltpu.VMEM((members, rows, LANES), F32),
            pltpu.VMEM((members, rows, LANES), F32),
            pltpu.VMEM((len(PAIRS), members, n_lev * count), F32),
            pltpu.VMEM((NB, n_lev, members // 2, LANES), F32),
            pltpu.VMEM((NB, n_lev - 1, members // 2, LANES), F32),
            pltpu.VMEM((NB - 1, n_lev, 8, LANES), F32),
            pltpu.VMEM((NB - 1, n_lev - 1, 8, LANES), F32),
            pair, pair, pair, pair, pair,
            pltpu.SemaphoreType.DMA((NB, 2)),
            pltpu.SemaphoreType.DMA((NB - 1, 2)),
        ],
        compiler_params=pltpu.CompilerParams(has_side_effects=True, vmem_limit_bytes=40 * 1024 * 1024),
    )(obs_owner, channel_weights, x, obs_offset, obs_value, obs_error, ancestors.reshape(NB, 1, members))
    return out.reshape(slab, tiles, depth, LANES).transpose(0, 2, 1, 3).reshape(slab, depth, cells)


def solution(mesh):
    in_specs = (
        P("grid", "lev", None),
        P("lev", None),
        P(),
        P(),
        P(None, "lev", None),
        P(None, "lev", None),
        P(None, "lev", "grid", None),
    )
    out_specs = P("grid", "lev", None)
    step = functools.partial(body, mesh.shape["grid"], mesh.shape["lev"])
    return jax.shard_map(step, mesh=mesh, in_specs=in_specs, out_specs=out_specs, check_vma=False)
```

time: 1160 us -> 72.8 us (0.06)
  waiting for transfers between devices: 878 us -> 0 us
  local copies, waits for them, and re-layouts: 179 us -> 4.59 us
  Pallas kernels: 0 us -> 68 us
  blocking collectives: 30.3 us -> 0 us
  between operations: 21.8 us -> 0.02 us
  other arithmetic: 18.7 us -> 0 us
  starting transfers between devices: 13.7 us -> 0 us
    psum x8 -> x0, waiting for transfers between devices: 862 us -> none  [the longest x4 696 us: spread(): return lax.psum(kept, axis)]
    unnamed x18 -> x15, local copies, waits for them, and re-layouts: 136 us -> 4.59 us
    pallas_call x0 -> x1, Pallas kernels: none -> 68 us  [body(): pl.pallas_call(functools.partial(kernel, n_grid, n_lev), out_shape=jax.Sh...]
    all_to_all x5 -> x0, local copies, waits for them, and re-layouts: 37.6 us -> none  [the longest x4 36.7 us: body(): lax.all_to_all(prior_fields, 'grid', split_axis=2, concat_axis=0, tiled=T...]
    all_to_all x1 -> x0, blocking collectives: 30.3 us -> none  [body(): lax.all_to_all(fields, 'grid', split_axis=0, concat_axis=2, tiled=True)]
    all_to_all x1 -> x0, waiting for transfers between devices: 16.1 us -> none  [body(): lax.all_to_all(prior_fields, 'grid', split_axis=2, concat_axis=0, tiled=T...]
    all_to_all x1 -> x0, starting transfers between devices: 13.2 us -> none  [body(): lax.all_to_all(prior_fields, 'grid', split_axis=2, concat_axis=0, tiled=T...]
  transfers between devices with their start and end apart: 9 -> 0, of which waited for: 9 -> 0; matrix products, arithmetic and copies ran while one was open for 0% -> 0% of each run, Pallas kernels for 0% -> 0%
where the time goes in v1:
time: 72.8 us; the launch traced here: 72.6 us
  Pallas kernels  68 us (93%)
  local copies, waits for them, and re-layouts  4.59 us (6%)
    pallas_call x1, Pallas kernels, body(): pl.pallas_call(functools.partial(kernel, n_grid, n_lev), out_shape=jax.Sh...  68 us
    unnamed x15, local copies, waits for them, and re-layouts  4.59 us

profile of v1, /device:TPU:1, one launch (start us, length us, event | category | flops | bytes accessed | tf_op | source)
XLA Modules:
  0.0 72.6 jit_solution(2314625622943603294)
XLA Ops:
  0.0 0.0 copy-start.2
  0.0 0.0 copy-start.5
  0.0 0.0 copy-start.6
  0.0 0.7 copy-done.2
  0.7 0.0 copy-done.5
  0.7 0.0 copy-done.6
  0.7 0.0 copy-start
  0.7 1.0 %copy-done = f32[2,2,32768]{2,1,0:T(2,128)S(1)} copy-done((f32[2,2,32768]{2,1,0:T(2,128)S(1)}, f32[2,2,32768]{2,1,0:T(2,128)}, u32[]{:S(2)}) %copy-start) | copy-done | bytes 524312
  1.7 0.0 copy-start.1
  1.7 0.7 copy-done.1
  2.4 0.0 copy-start.3
  2.4 0.7 copy-done.3
  3.1 0.0 copy-start.4
  3.1 0.7 copy-done.4
  3.8 68.0 %shard_map.73 = f32[2,512,128]{2,1,0:T(8,128)S(1)} custom-call(s32[4]{0:T(128)S(1)} %copy-done.6, f32[2,4]{1,0:T(2,128)S(1)} %copy-done.5, f32[2,512,128]{2,1,0:T(8,128)S(1)} %bitcast.12, s32[4,4,64]{2,1,0:T(4,128)S(1)} %copy-done.1, f32[4,1,64]{2,1,0:T(1,128)S(1)} %copy-done.2, f32[4,1,64]{2,1,0:T(1,128)S(1)} %copy-done.3, s32[4,1,128]{2,1,0:T(1,128)S(1)} %bitcast.13), custom_call_target="tpu_custom_call" | custom-call | tf_op jit(solution)/shard_map/pallas_call | solution.py:292
  71.8 0.8 %copy.11 = f32[2,2,32768]{2,1,0:T(2,128)} copy(f32[2,2,32768]{2,1,0:T(2,128)S(1)} %bitcast.11) | data formatting | bytes 1048576
Async XLA Ops:
  0.0 0.7 copy-start.2
  0.0 0.7 copy-start.5
  0.0 0.7 copy-start.6
  0.7 1.0 %copy-start = (f32[2,2,32768]{2,1,0:T(2,128)S(1)}, f32[2,2,32768]{2,1,0:T(2,128)}, u32[]{:S(2)}) copy-start(f32[2,2,32768]{2,1,0:T(2,128)} %param.7) | copy-start | bytes 1572868
  1.7 0.7 copy-start.1
  2.4 0.7 copy-start.3
  3.1 0.7 copy-start.4

commit v2 on v1

v2 whole, which is shorter than its diff:
```python
import functools

import jax
import jax.numpy as jnp
from jax import lax
from jax.experimental import pallas as pl
from jax.experimental.pallas import tpu as pltpu
from jax.sharding import PartitionSpec as P

NB = 4
LANES = 128
F32 = jnp.float32
BF16 = jnp.bfloat16
MESH = pl.DeviceIdType.MESH
BASE_ROW = (0, 8, 12, 16)
PAIRS = [(1, 0), (2, 0), (2, 1), (3, 0), (3, 1), (3, 2)]


def iota(shape, axis):
    return lax.broadcasted_iota(jnp.int32, shape, axis)


def split3(v):
    hi = v.astype(BF16)
    rest = v - hi.astype(F32)
    mid = rest.astype(BF16)
    low = (rest - mid.astype(F32)).astype(BF16)
    return hi, mid, low


def dot(a, b):
    return jnp.dot(a, b, preferred_element_type=F32)


def pick_dot(onehot, v):
    hi, mid, low = split3(v)
    return (dot(onehot, low) + dot(onehot, mid)) + dot(onehot, hi)


def kernel(
    n_grid, n_lev, owner_h, cw_h, x_h, off_h, val_h, err_h, anc_h, out,
    owner, cw, x, off, val, err, anc, pay, zbuf, first, picks, gath, f, y, ys, ssend, srecv, csend, crecv, tiles_s,
    load_sem, z_sem, f_sem, p_sem, g_sem, in_sem, out_sem, s_sem, r_sem,
):
    slab = x.shape[0]
    rows = x.shape[1] // n_grid
    members = slab * n_grid
    half = members // 2
    count = off.shape[2]
    block = rows * LANES // 2
    n_core, n_y = 2, 4
    n_z = n_grid // (n_core * n_y)
    n_col = n_core * n_y
    scale = n_grid / 2.0

    me = lax.axis_index("grid")
    lev = lax.axis_index("lev")
    core = me % n_core
    yy = (me // n_core) % n_y
    zz = me // n_col

    def slot_of(g):
        return (g % n_core) * (n_y * n_z) + ((g // n_core) % n_y) * n_z + g // n_col

    def grid_of(s):
        return ((s % n_z) * n_y + (s // n_z) % n_y) * n_core + s // (n_z * n_y)

    my_slot = slot_of(me)
    my_col = core * n_y + yy

    def col_peer(d):
        return zz * n_col + (me + d) % n_col

    loads = []
    for k, (src, dst) in enumerate(
        [(x_h, x), (owner_h, owner), (off_h, off), (cw_h, cw), (anc_h, anc), (val_h, val), (err_h, err)]
    ):
        copy = pltpu.make_async_copy(src, dst, load_sem.at[k])
        copy.start()
        loads.append(copy)

    barrier = pltpu.get_barrier_semaphore()

    def hello(grid, level):
        pl.semaphore_signal(barrier, inc=1, device_id=(grid, level), device_id_type=MESH)

    for d in range(1, n_z):
        hello((me + d * n_col) % n_grid, lev)
    for e in range(n_lev):
        for d in range(n_col):
            if d or e:
                hello(col_peer(d), (lev + e) % n_lev)

    def send(src, dst, sem, grid, level):
        pltpu.make_async_remote_copy(
            src_ref=src, dst_ref=dst, send_sem=sem.at[0], recv_sem=sem.at[1],
            device_id=(grid, level), device_id_type=MESH,
        ).start()

    def drain(ref, sem):
        pltpu.make_async_copy(ref, ref, sem).wait()

    for copy in loads:
        copy.wait()

    lane256 = iota((1, n_lev * count), 1)
    wrow = []
    for level in range(2):
        w = jnp.zeros((1, n_lev * count), F32)
        for g in range(n_lev):
            w = jnp.where(lane256 // count == g, cw[level, g], w)
        wrow.append(w)
    row16 = iota((slab * rows, n_lev * count), 0)
    weights = jnp.where(row16 % 2 == 0, wrow[0], wrow[1])
    tile_of_row = (row16 % rows) // 2

    def scan_blocks(k, tiles):
        tile = x[:, pl.ds(pl.multiple_of(k * rows, rows), rows), :]
        return tuple(jnp.where(owner[b] == k, tile, kept) for b, kept in enumerate(tiles))

    zero = jnp.zeros((slab, rows, LANES), F32)
    tiles = lax.fori_loop(0, n_grid, scan_blocks, (zero,) * NB, unroll=8)
    pay[...] = jnp.zeros_like(pay)
    for b in range(NB):
        src = tiles[b].reshape(slab * rows, LANES)
        cells = jnp.concatenate([off[b, g : g + 1, :] for g in range(n_lev)], axis=1)
        onehot = (iota((LANES, n_lev * count), 0) == cells % LANES).astype(BF16)
        hi, mid, low = split3(src)
        got = (dot(low, onehot) + dot(mid, onehot)) + dot(hi, onehot)
        got = jnp.where(tile_of_row == cells // LANES, got * weights, 0.0)
        for i in range(slab):
            value = jnp.sum(got[i * rows : (i + 1) * rows], axis=0, keepdims=True)
            for h in range(2):
                at = BASE_ROW[b] + h * 2 + i
                pay[at : at + 1, :] = value[:, h * LANES : (h + 1) * LANES]
        if b < NB - 1:
            pay[4 + b : 5 + b, :] = anc[b].astype(F32)

    pl.semaphore_wait(barrier, n_z - 1 + n_lev * n_col - 1)

    for d in range(1, n_z):
        send(pay, zbuf.at[zz], z_sem, (me + d * n_col) % n_grid, lev)
    zbuf[zz] = pay[...]

    lane1 = iota((1, LANES), 1)
    low8 = iota((n_z, LANES), 1) < count
    member_lane = iota((members, members), 1)
    eye = (iota((members, members), 0) == member_lane).astype(F32)

    taper = {}
    alpha = {}
    for b in range(NB):
        cells = off[b, pl.ds(lev, 1), :]
        where = (owner[b] * block + cells).astype(F32) / block
        where = jnp.concatenate([where, where], axis=1)
        regions = {0: me}
        for later in range(b + 1, NB):
            regions[later] = owner[later]
        for key, region in regions.items():
            distance = ((region.astype(F32) + 0.5) - where) / scale
            t = jnp.exp(-0.5 * distance * distance)
            taper[b, key] = t
            total = jnp.sum(t, axis=1, keepdims=True)
            alpha[b, key] = 0.8 * (1.0 - jnp.exp(-total / (2 * count)))

    drain(zbuf.at[pl.ds(0, n_z - 1)], z_sem.at[1])
    z2 = zbuf.reshape(n_z * 24, LANES)
    for g in range(n_lev):
        a = z2[pl.ds((g // 2) * 2, n_z, stride=24), :]
        c = z2[pl.ds((g // 2) * 2 + 1, n_z, stride=24), :]
        tiles_s[g] = jnp.where(low8, a, pltpu.roll(c, count, 1)) if g % 2 == 0 else jnp.where(low8, pltpu.roll(a, count, 1), c)
    for e in range(n_lev):
        level = (lev + e) % n_lev
        for d in range(n_col):
            if d or e:
                send(tiles_s.at[level], first.at[lev * n_col + my_col], f_sem, col_peer(d), level)
    first[lev * n_col + my_col] = tiles_s[lev]

    z_of_row = iota((n_z, LANES), 0)
    rows_of = [z2[pl.ds(4 + i, n_z, stride=24), :] for i in range(NB - 1)]
    found = [
        jnp.sum(jnp.where(z_of_row * n_col + yy * n_core + core == owner[b], rows_of[i], 0.0), axis=0, keepdims=True)
        for b, i in PAIRS
    ]
    tiles_s[n_lev] = jnp.concatenate(found + found[:2], axis=0)
    for d in range(1, n_col):
        send(tiles_s.at[n_lev], picks.at[my_col], p_sem, col_peer(d), lev)
    picks[my_col] = tiles_s[n_lev]
    for k in range(2):
        mine = zbuf.at[:, pl.ds(8 + 8 * k, 8), :]
        for d in range(1, n_col):
            send(mine, gath.at[k, pl.ds(my_col * n_z, n_z)], g_sem.at[k], col_peer(d), lev)
        gath[k, pl.ds(my_col * n_z, n_z)] = zbuf[:, 8 + 8 * k : 16 + 8 * k, :]

    def push_in(t, carry):
        peer = (me + t) % n_grid
        send(
            x.at[:, pl.ds(pl.multiple_of(peer * rows, rows), rows), :],
            f.at[pl.ds(my_slot * slab, slab)],
            in_sem, peer, lev,
        )
        return carry

    lax.fori_loop(1, n_grid, push_in, 0)
    f[pl.ds(my_slot * slab, slab)] = x[:, pl.ds(pl.multiple_of(me * rows, rows), rows), :]

    sub = iota((members, members), 0)
    perm = (grid_of(sub % n_grid) * slab + sub // n_grid == member_lane).astype(BF16)

    def columns(stack):
        stack = stack.astype(jnp.int32)
        stack = (slot_of(stack // slab) + (stack % slab) * n_grid).astype(F32).astype(BF16)
        return lax.dot_general(perm, stack, (((1,), (1,)), ((), ())), preferred_element_type=F32)

    def picker(cols, k):
        return (cols[:, k : k + 1].astype(jnp.int32) == member_lane).astype(BF16)

    own = [anc[b].astype(F32) for b in range(NB)]
    own_cols = columns(jnp.concatenate(own + own, axis=0))
    chain = [eye]
    for b in range(NB):
        a = alpha[b, 0]
        chosen = picker(own_cols, b)
        moved = chosen.astype(F32) if b == 0 else pick_dot(chosen, chain[b])
        chain.append(a * moved + (1.0 - a) * chain[b])

    low_half = iota((half, LANES), 1) < count
    shift = {b: jnp.zeros((1, n_lev * count), F32) for b in range(1, NB)}
    mean_row = jnp.zeros((1, members), F32)

    def exchange_base(b, v):
        top, bottom = v[:half], v[half:]
        for g in range(n_lev):
            lanes = slice((g // 2) * LANES, (g // 2 + 1) * LANES)
            a, c = top[:, lanes], bottom[:, lanes]
            if g % 2 == 0:
                packed = jnp.where(low_half, a, pltpu.roll(c, count, 1))
            else:
                packed = jnp.where(low_half, pltpu.roll(a, count, 1), c)
            ssend[b - 1, g] = packed
        for d in range(1, n_lev):
            level = (lev + d) % n_lev
            send(ssend.at[b - 1, level], srecv.at[b - 1, d - 1], s_sem.at[b - 1], me, level)

    def base(b, pair_cols):
        k, r = (b - 1) // 2, ((b - 1) % 2) * 4
        g2 = gath.reshape(2 * n_grid * 8, LANES)
        parts = []
        for h in range(2):
            two = [g2[pl.ds(k * n_grid * 8 + r + h * 2 + i, n_grid, stride=8), :] for i in range(slab)]
            parts.append(jnp.concatenate(two, axis=0))
        v = jnp.concatenate(parts, axis=1)
        for i in range(b):
            ys[PAIRS.index((b, i))] = v
            a = alpha[i, b]
            v = a * pick_dot(picker(pair_cols, PAIRS.index((b, i))), v) + (1.0 - a) * v
        exchange_base(b, v)

    def weigh(b, prior):
        row = jnp.zeros((1, members), F32)
        seen = jnp.concatenate([val[b], val[b]], axis=1)
        dev = jnp.concatenate([err[b], err[b]], axis=1)
        innovation = ((seen - prior) / dev) ** 2
        for key in list(range(b + 1, NB)) + [0]:
            weighted = innovation * taper[b, key]
            top = jnp.sum(jnp.where(low_half, weighted, 0.0), axis=1, keepdims=True)
            bottom = jnp.sum(jnp.where(low_half, 0.0, weighted), axis=1, keepdims=True)
            log_weight = (-0.5 / count) * jnp.concatenate([top, bottom], axis=0)
            expo = jnp.exp(log_weight - jnp.max(log_weight, axis=0, keepdims=True))
            change = expo / jnp.sum(expo, axis=0, keepdims=True) - 1.0 / members
            if key == 0:
                row = jnp.sum(change * chain[b], axis=0, keepdims=True)
            else:
                shift[key] = shift[key] + jnp.sum(change * ys[PAIRS.index((key, b))], axis=0, keepdims=True)
                if key == b + 1:
                    push_shift(key)
        return row

    def push_shift(b):
        for g in range(n_lev):
            row = shift[b][:, (g // 2) * LANES : (g // 2 + 1) * LANES]
            other = pltpu.roll(row, count, 1)
            left = lane1 < count
            row = jnp.where(left, row, other) if g % 2 == 0 else jnp.where(left, other, row)
            csend[b - 1, g] = jnp.broadcast_to(row, (8, LANES))
        for d in range(1, n_lev):
            level = (lev + d) % n_lev
            send(csend.at[b - 1, level], crecv.at[b - 1, d - 1], r_sem.at[b - 1], me, level)

    drain(picks.at[pl.ds(0, n_col - 1)], p_sem.at[1])
    chosen = picks[0]
    for k in range(1, n_col):
        chosen = chosen + picks[k]
    pair_cols = columns(chosen)
    drain(gath.at[0, pl.ds(0, (n_col - 1) * n_z)], g_sem.at[0, 1])
    base(1, pair_cols)
    base(2, pair_cols)
    drain(gath.at[1, pl.ds(0, (n_col - 1) * n_z)], g_sem.at[1, 1])
    base(3, pair_cols)

    drain(first.at[pl.ds(0, n_lev * n_col - 1)], f_sem.at[1])
    prior = first[:n_col]
    for level in range(1, n_lev):
        prior = prior + first[level * n_col : (level + 1) * n_col]
    mean_row = weigh(0, prior.reshape(half, LANES))
    for b in range(1, NB):
        drain(srecv.at[b - 1], s_sem.at[b - 1, 1])
        prior = ssend[b - 1, lev]
        for d in range(n_lev - 1):
            prior = prior + srecv[b - 1, d]
        drain(crecv.at[b - 1], r_sem.at[b - 1, 1])
        row = csend[b - 1, lev]
        for d in range(n_lev - 1):
            row = row + crecv[b - 1, d]
        mean_row = mean_row + weigh(b, prior + row[0:1, :])

    total = chain[NB] + mean_row
    t_hi, t_mid, t_low = split3(total)
    drain(f.at[pl.ds(0, members - slab)], in_sem.at[1])
    f2 = f.reshape(members * rows, LANES)
    y2 = y.reshape(members * rows, LANES)
    for s in range(rows):
        two = [f2[pl.ds(i * rows + s, n_grid, stride=slab * rows), :] for i in range(slab)]
        hi, mid, low = split3(jnp.concatenate(two, axis=0))
        mixed = (dot(t_low, hi) + dot(t_mid, mid)) + dot(t_hi, low)
        mixed = mixed + (dot(t_mid, hi) + dot(t_hi, mid))
        mixed = mixed + dot(t_hi, hi)
        for i in range(slab):
            y2[pl.ds(i * rows + s, n_grid, stride=slab * rows), :] = mixed[i * n_grid : (i + 1) * n_grid]

    def push_out(t, carry):
        peer = (me + t) % n_grid
        send(
            y.at[pl.ds(slot_of(peer) * slab, slab)],
            out.at[:, pl.ds(pl.multiple_of(me * rows, rows), rows), :],
            out_sem, peer, lev,
        )
        return carry

    lax.fori_loop(1, n_grid, push_out, 0)
    keep = pltpu.make_async_copy(
        y.at[pl.ds(my_slot * slab, slab)], out.at[:, pl.ds(pl.multiple_of(me * rows, rows), rows), :], load_sem.at[0]
    )
    keep.start()
    keep.wait()

    drain(zbuf.at[pl.ds(0, n_z - 1)], z_sem.at[0])
    drain(first.at[pl.ds(0, n_lev * n_col - 1)], f_sem.at[0])
    drain(picks.at[pl.ds(0, n_col - 1)], p_sem.at[0])
    for k in range(2):
        drain(gath.at[0, pl.ds(0, (n_col - 1) * n_z)], g_sem.at[k, 0])
    drain(f.at[pl.ds(0, members - slab)], in_sem.at[0])
    for b in range(NB - 1):
        drain(srecv.at[b], s_sem.at[b, 0])
        drain(crecv.at[b], r_sem.at[b, 0])
    drain(y.at[pl.ds(0, members - slab)], out_sem.at[1])
    drain(y.at[pl.ds(0, members - slab)], out_sem.at[0])


def body(n_grid, n_lev, prior_fields, channel_weights, obs_owner, obs_offset, obs_value, obs_error, ancestors):
    slab, depth, cells = prior_fields.shape
    tiles = cells // LANES
    x = prior_fields.reshape(slab, depth, tiles, LANES).transpose(0, 2, 1, 3).reshape(slab, tiles * depth, LANES)
    members = slab * n_grid
    rows = tiles * depth // n_grid
    count = obs_offset.shape[2]
    n_col = 8
    n_z = n_grid // n_col
    vm = pl.BlockSpec(memory_space=pltpu.VMEM)
    hbm = pl.BlockSpec(memory_space=pltpu.HBM)
    pair = pltpu.SemaphoreType.DMA((2,))
    out = pl.pallas_call(
        functools.partial(kernel, n_grid, n_lev),
        out_shape=jax.ShapeDtypeStruct((slab, tiles * depth, LANES), F32),
        in_specs=[hbm] * 7,
        out_specs=hbm,
        scratch_shapes=[
            pltpu.SMEM(obs_owner.shape, jnp.int32),
            pltpu.SMEM(channel_weights.shape, F32),
            pltpu.VMEM(x.shape, F32),
            pltpu.VMEM(obs_offset.shape, jnp.int32),
            pltpu.VMEM(obs_value.shape, F32),
            pltpu.VMEM(obs_error.shape, F32),
            pltpu.VMEM((NB, 1, members), jnp.int32),
            pltpu.VMEM((24, LANES), F32),
            pltpu.VMEM((n_z, 24, LANES), F32),
            pltpu.VMEM((n_lev * n_col, n_z, LANES), F32),
            pltpu.VMEM((n_col, 8, LANES), F32),
            pltpu.VMEM((2, n_grid, 8, LANES), F32),
            pltpu.VMEM((members, rows, LANES), F32),
            pltpu.VMEM((members, rows, LANES), F32),
            pltpu.VMEM((len(PAIRS), members, n_lev * count), F32),
            pltpu.VMEM((NB - 1, n_lev, members // 2, LANES), F32),
            pltpu.VMEM((NB - 1, n_lev - 1, members // 2, LANES), F32),
            pltpu.VMEM((NB - 1, n_lev, 8, LANES), F32),
            pltpu.VMEM((NB - 1, n_lev - 1, 8, LANES), F32),
            pltpu.VMEM((n_lev + 1, 8, LANES), F32),
            pltpu.SemaphoreType.DMA((7,)),
            pair, pair, pair,
            pltpu.SemaphoreType.DMA((2, 2)),
            pair, pair,
            pltpu.SemaphoreType.DMA((NB - 1, 2)),
            pltpu.SemaphoreType.DMA((NB - 1, 2)),
        ],
        compiler_params=pltpu.CompilerParams(
            has_side_effects=True, collective_id=0, vmem_limit_bytes=56 * 1024 * 1024
        ),
    )(obs_owner, channel_weights, x, obs_offset, obs_value, obs_error, ancestors.reshape(NB, 1, members))
    return out.reshape(slab, tiles, depth, LANES).transpose(0, 2, 1, 3).reshape(slab, depth, cells)


def solution(mesh):
    in_specs = (
        P("grid", "lev", None),
        P("lev", None),
        P(),
        P(),
        P(None, "lev", None),
        P(None, "lev", None),
        P(None, "lev", "grid", None),
    )
    out_specs = P("grid", "lev", None)
    step = functools.partial(body, mesh.shape["grid"], mesh.shape["lev"])
    return jax.shard_map(step, mesh=mesh, in_specs=in_specs, out_specs=out_specs, check_vma=False)
```

time: 72.8 us -> 57.5 us (0.79)
  Pallas kernels: 68 us -> 55.5 us
  local copies, waits for them, and re-layouts: 4.59 us -> 1.87 us
    pallas_call x1, Pallas kernels: 68 us -> 55.5 us  [body(): pl.pallas_call(functools.partial(kernel, n_grid, n_lev), out_shape=jax.Sh...]
    unnamed x15 -> x1, local copies, waits for them, and re-layouts: 4.59 us -> 1.87 us
where the time goes in v2:
time: 57.5 us; the launch traced here: 57.3 us
  Pallas kernels  55.5 us (97%)
  local copies, waits for them, and re-layouts  1.87 us (3%)
    pallas_call x1, Pallas kernels, body(): pl.pallas_call(functools.partial(kernel, n_grid, n_lev), out_shape=jax.Sh...  55.5 us
    unnamed x1, local copies, waits for them, and re-layouts  1.87 us

profile of v2, /device:TPU:1, one launch (start us, length us, event | category | flops | bytes accessed | tf_op | source)
XLA Modules:
  0.0 57.3 jit_solution(4367529124107895485)
XLA Ops:
  0.0 55.5 %shard_map.73 = f32[2,512,128]{2,1,0:T(8,128)} custom-call(s32[4]{0:T(128)} %owner_h.1, f32[2,4]{1,0:T(2,128)} %cw_h.1, f32[2,512,128]{2,1,0:T(8,128)} %bitcast.12, s32[4,4,64]{2,1,0:T(4,128)} %off_h.1, f32[4,1,64]{2,1,0:T(1,128)} %val_h.1, f32[4,1,64]{2,1,0:T(1,128)} %err_h.1, s32[4,1,128]{2,1,0:T(1,128)} %bitcast.13), custom_call_target="tpu_custom_call" | custom-call | tf_op jit(solution)/shard_map/pallas_call | solution.py:372
  55.5 1.9 %copy.11 = f32[2,2,32768]{2,1,0:T(2,128)} copy(f32[2,2,32768]{2,1,0:T(2,128)} %bitcast.11) | data formatting | bytes 1048576

commit v3 on v2

--- a/solution.py
+++ b/solution.py
@@ -13,6 +13,8 @@
 BF16 = jnp.bfloat16
 MESH = pl.DeviceIdType.MESH
 BASE_ROW = (0, 8, 12, 16)
+BATCH_TILE = 5
+CUTS = (1, 64, 64, 64, 64, 64, 64, 64)
 PAIRS = [(1, 0), (2, 0), (2, 1), (3, 0), (3, 1), (3, 2)]
 
 
@@ -163,6 +165,26 @@
             total = jnp.sum(t, axis=1, keepdims=True)
             alpha[b, key] = 0.8 * (1.0 - jnp.exp(-total / (2 * count)))
 
+    sub = iota((members, members), 0)
+    perm = (grid_of(sub % n_grid) * slab + sub // n_grid == member_lane).astype(BF16)
+
+    def columns(stack):
+        stack = stack.astype(jnp.int32)
+        stack = (slot_of(stack // slab) + (stack % slab) * n_grid).astype(F32).astype(BF16)
+        return lax.dot_general(perm, stack, (((1,), (1,)), ((), ())), preferred_element_type=F32)
+
+    def picker(cols, k):
+        return (cols[:, k : k + 1].astype(jnp.int32) == member_lane).astype(BF16)
+
+    own = [anc[b].astype(F32) for b in range(NB)]
+    own_cols = columns(jnp.concatenate(own + own, axis=0))
+    chain = [eye]
+    for b in range(NB):
+        a = alpha[b, 0]
+        chosen = picker(own_cols, b)
+        moved = chosen.astype(F32) if b == 0 else pick_dot(chosen, chain[b])
+        chain.append(a * moved + (1.0 - a) * chain[b])
+
     drain(zbuf.at[pl.ds(0, n_z - 1)], z_sem.at[1])
     z2 = zbuf.reshape(n_z * 24, LANES)
     for g in range(n_lev):
@@ -186,14 +208,17 @@
     for d in range(1, n_col):
         send(tiles_s.at[n_lev], picks.at[my_col], p_sem, col_peer(d), lev)
     picks[my_col] = tiles_s[n_lev]
-    for k in range(2):
-        mine = zbuf.at[:, pl.ds(8 + 8 * k, 8), :]
+    for b in range(1, NB):
+        for r in range(4):
+            tiles_s[BATCH_TILE + 4 * (b - 1) + r] = z2[pl.ds(BASE_ROW[b] + r, n_z, stride=24), :]
+        mine = tiles_s.at[pl.ds(BATCH_TILE + 4 * (b - 1), 4)]
         for d in range(1, n_col):
-            send(mine, gath.at[k, pl.ds(my_col * n_z, n_z)], g_sem.at[k], col_peer(d), lev)
-        gath[k, pl.ds(my_col * n_z, n_z)] = zbuf[:, 8 + 8 * k : 16 + 8 * k, :]
+            send(mine, gath.at[b - 1, my_col], g_sem.at[b - 1], col_peer(d), lev)
+        gath[b - 1, my_col] = tiles_s[BATCH_TILE + 4 * (b - 1) : BATCH_TILE + 4 * b]
 
     def push_in(t, carry):
-        peer = (me + t) % n_grid
+        far = (t + 1) // 2
+        peer = (me + far + (1 - t % 2) * (n_grid - 2 * far)) % n_grid
         send(
             x.at[:, pl.ds(pl.multiple_of(peer * rows, rows), rows), :],
             f.at[pl.ds(my_slot * slab, slab)],
@@ -201,32 +226,14 @@
         )
         return carry
 
-    lax.fori_loop(1, n_grid, push_in, 0)
+    def push_blocks(k):
+        lax.fori_loop(CUTS[k], CUTS[k + 1], push_in, 0)
+
+    push_blocks(0)
     f[pl.ds(my_slot * slab, slab)] = x[:, pl.ds(pl.multiple_of(me * rows, rows), rows), :]
-
-    sub = iota((members, members), 0)
-    perm = (grid_of(sub % n_grid) * slab + sub // n_grid == member_lane).astype(BF16)
-
-    def columns(stack):
-        stack = stack.astype(jnp.int32)
-        stack = (slot_of(stack // slab) + (stack % slab) * n_grid).astype(F32).astype(BF16)
-        return lax.dot_general(perm, stack, (((1,), (1,)), ((), ())), preferred_element_type=F32)
-
-    def picker(cols, k):
-        return (cols[:, k : k + 1].astype(jnp.int32) == member_lane).astype(BF16)
-
-    own = [anc[b].astype(F32) for b in range(NB)]
-    own_cols = columns(jnp.concatenate(own + own, axis=0))
-    chain = [eye]
-    for b in range(NB):
-        a = alpha[b, 0]
-        chosen = picker(own_cols, b)
-        moved = chosen.astype(F32) if b == 0 else pick_dot(chosen, chain[b])
-        chain.append(a * moved + (1.0 - a) * chain[b])
 
     low_half = iota((half, LANES), 1) < count
     shift = {b: jnp.zeros((1, n_lev * count), F32) for b in range(1, NB)}
-    mean_row = jnp.zeros((1, members), F32)
 
     def exchange_base(b, v):
         top, bottom = v[:half], v[half:]
@@ -242,14 +249,14 @@
             level = (lev + d) % n_lev
             send(ssend.at[b - 1, level], srecv.at[b - 1, d - 1], s_sem.at[b - 1], me, level)
 
-    def base(b, pair_cols):
-        k, r = (b - 1) // 2, ((b - 1) % 2) * 4
-        g2 = gath.reshape(2 * n_grid * 8, LANES)
+    def member_values(b):
         parts = []
         for h in range(2):
-            two = [g2[pl.ds(k * n_grid * 8 + r + h * 2 + i, n_grid, stride=8), :] for i in range(slab)]
+            two = [gath[b - 1, :, h * 2 + i].reshape(n_grid, LANES) for i in range(slab)]
             parts.append(jnp.concatenate(two, axis=0))
-        v = jnp.concatenate(parts, axis=1)
+        return jnp.concatenate(parts, axis=1)
+
+    def base(b, v, pair_cols):
         for i in range(b):
             ys[PAIRS.index((b, i))] = v
             a = alpha[i, b]
@@ -257,24 +264,21 @@
         exchange_base(b, v)
 
     def weigh(b, prior):
-        row = jnp.zeros((1, members), F32)
         seen = jnp.concatenate([val[b], val[b]], axis=1)
         dev = jnp.concatenate([err[b], err[b]], axis=1)
         innovation = ((seen - prior) / dev) ** 2
+        changes = {}
         for key in list(range(b + 1, NB)) + [0]:
             weighted = innovation * taper[b, key]
             top = jnp.sum(jnp.where(low_half, weighted, 0.0), axis=1, keepdims=True)
             bottom = jnp.sum(jnp.where(low_half, 0.0, weighted), axis=1, keepdims=True)
             log_weight = (-0.5 / count) * jnp.concatenate([top, bottom], axis=0)
             expo = jnp.exp(log_weight - jnp.max(log_weight, axis=0, keepdims=True))
-            change = expo / jnp.sum(expo, axis=0, keepdims=True) - 1.0 / members
-            if key == 0:
-                row = jnp.sum(change * chain[b], axis=0, keepdims=True)
-            else:
-                shift[key] = shift[key] + jnp.sum(change * ys[PAIRS.index((key, b))], axis=0, keepdims=True)
-                if key == b + 1:
-                    push_shift(key)
-        return row
+            changes[key] = expo / jnp.sum(expo, axis=0, keepdims=True) - 1.0 / members
+        return changes
+
+    def move(b, change, v):
+        shift[b] = shift[b] + jnp.sum(change * v, axis=0, keepdims=True)
 
     def push_shift(b):
         for g in range(n_lev):
@@ -287,23 +291,7 @@
             level = (lev + d) % n_lev
             send(csend.at[b - 1, level], crecv.at[b - 1, d - 1], r_sem.at[b - 1], me, level)
 
-    drain(picks.at[pl.ds(0, n_col - 1)], p_sem.at[1])
-    chosen = picks[0]
-    for k in range(1, n_col):
-        chosen = chosen + picks[k]
-    pair_cols = columns(chosen)
-    drain(gath.at[0, pl.ds(0, (n_col - 1) * n_z)], g_sem.at[0, 1])
-    base(1, pair_cols)
-    base(2, pair_cols)
-    drain(gath.at[1, pl.ds(0, (n_col - 1) * n_z)], g_sem.at[1, 1])
-    base(3, pair_cols)
-
-    drain(first.at[pl.ds(0, n_lev * n_col - 1)], f_sem.at[1])
-    prior = first[:n_col]
-    for level in range(1, n_lev):
-        prior = prior + first[level * n_col : (level + 1) * n_col]
-    mean_row = weigh(0, prior.reshape(half, LANES))
-    for b in range(1, NB):
+    def full_prior(b):
         drain(srecv.at[b - 1], s_sem.at[b - 1, 1])
         prior = ssend[b - 1, lev]
         for d in range(n_lev - 1):
@@ -312,7 +300,42 @@
         row = csend[b - 1, lev]
         for d in range(n_lev - 1):
             row = row + crecv[b - 1, d]
-        mean_row = mean_row + weigh(b, prior + row[0:1, :])
+        return prior + row[0:1, :]
+
+    drain(first.at[pl.ds(0, n_lev * n_col - 1)], f_sem.at[1])
+    prior = first[:n_col]
+    for level in range(1, n_lev):
+        prior = prior + first[level * n_col : (level + 1) * n_col]
+    change = {0: weigh(0, prior.reshape(half, LANES))}
+    push_blocks(1)
+
+    drain(picks.at[pl.ds(0, n_col - 1)], p_sem.at[1])
+    chosen = picks[0]
+    for k in range(1, n_col):
+        chosen = chosen + picks[k]
+    pair_cols = columns(chosen)
+    for b in range(1, NB):
+        drain(gath.at[b - 1, pl.ds(0, n_col - 1)], g_sem.at[b - 1, 1])
+        v = member_values(b)
+        if b == 1:
+            move(1, change[0][1], v)
+            base(1, v, pair_cols)
+            push_shift(1)
+            push_blocks(2)
+        else:
+            base(b, v, pair_cols)
+            move(b, change[0][b], v)
+    push_blocks(3)
+    for b in range(1, NB):
+        change[b] = weigh(b, full_prior(b))
+        for later in range(b + 1, NB):
+            move(later, change[b][later], ys[PAIRS.index((later, b))])
+            if later == b + 1:
+                push_shift(later)
+        push_blocks(3 + b)
+    mean_row = jnp.zeros((1, members), F32)
+    for b in range(NB):
+        mean_row = mean_row + jnp.sum(change[b][0] * chain[b], axis=0, keepdims=True)
 
     total = chain[NB] + mean_row
     t_hi, t_mid, t_low = split3(total)
@@ -338,17 +361,13 @@
         return carry
 
     lax.fori_loop(1, n_grid, push_out, 0)
-    keep = pltpu.make_async_copy(
-        y.at[pl.ds(my_slot * slab, slab)], out.at[:, pl.ds(pl.multiple_of(me * rows, rows), rows), :], load_sem.at[0]
-    )
-    keep.start()
-    keep.wait()
+    out[:, pl.ds(pl.multiple_of(me * rows, rows), rows), :] = y[pl.ds(my_slot * slab, slab)]
 
     drain(zbuf.at[pl.ds(0, n_z - 1)], z_sem.at[0])
     drain(first.at[pl.ds(0, n_lev * n_col - 1)], f_sem.at[0])
     drain(picks.at[pl.ds(0, n_col - 1)], p_sem.at[0])
-    for k in range(2):
-        drain(gath.at[0, pl.ds(0, (n_col - 1) * n_z)], g_sem.at[k, 0])
+    for b in range(NB - 1):
+        drain(gath.at[b, pl.ds(0, n_col - 1)], g_sem.at[b, 0])
     drain(f.at[pl.ds(0, members - slab)], in_sem.at[0])
     for b in range(NB - 1):
         drain(srecv.at[b], s_sem.at[b, 0])
@@ -369,11 +388,12 @@
     vm = pl.BlockSpec(memory_space=pltpu.VMEM)
     hbm = pl.BlockSpec(memory_space=pltpu.HBM)
     pair = pltpu.SemaphoreType.DMA((2,))
+    arrays = (obs_owner, channel_weights, x, obs_offset, obs_value, obs_error, ancestors.reshape(NB, 1, members))
     out = pl.pallas_call(
         functools.partial(kernel, n_grid, n_lev),
         out_shape=jax.ShapeDtypeStruct((slab, tiles * depth, LANES), F32),
         in_specs=[hbm] * 7,
-        out_specs=hbm,
+        out_specs=vm,
         scratch_shapes=[
             pltpu.SMEM(obs_owner.shape, jnp.int32),
             pltpu.SMEM(channel_weights.shape, F32),
@@ -386,7 +406,7 @@
             pltpu.VMEM((n_z, 24, LANES), F32),
             pltpu.VMEM((n_lev * n_col, n_z, LANES), F32),
             pltpu.VMEM((n_col, 8, LANES), F32),
-            pltpu.VMEM((2, n_grid, 8, LANES), F32),
+            pltpu.VMEM((NB - 1, n_col, 4, n_z, LANES), F32),
             pltpu.VMEM((members, rows, LANES), F32),
             pltpu.VMEM((members, rows, LANES), F32),
             pltpu.VMEM((len(PAIRS), members, n_lev * count), F32),
@@ -394,18 +414,18 @@
             pltpu.VMEM((NB - 1, n_lev - 1, members // 2, LANES), F32),
             pltpu.VMEM((NB - 1, n_lev, 8, LANES), F32),
             pltpu.VMEM((NB - 1, n_lev - 1, 8, LANES), F32),
-            pltpu.VMEM((n_lev + 1, 8, LANES), F32),
+            pltpu.VMEM((BATCH_TILE + 4 * (NB - 1), 8, LANES), F32),
             pltpu.SemaphoreType.DMA((7,)),
             pair, pair, pair,
-            pltpu.SemaphoreType.DMA((2, 2)),
+            pltpu.SemaphoreType.DMA((NB - 1, 2)),
             pair, pair,
             pltpu.SemaphoreType.DMA((NB - 1, 2)),
             pltpu.SemaphoreType.DMA((NB - 1, 2)),
         ],
         compiler_params=pltpu.CompilerParams(
-            has_side_effects=True, collective_id=0, vmem_limit_bytes=56 * 1024 * 1024
+            has_side_effects=True, collective_id=0, vmem_limit_bytes=24 * 1024 * 1024
         ),
-    )(obs_owner, channel_weights, x, obs_offset, obs_value, obs_error, ancestors.reshape(NB, 1, members))
+    )(*[pltpu.with_memory_space_constraint(v, pltpu.HBM) for v in arrays])
     return out.reshape(slab, tiles, depth, LANES).transpose(0, 2, 1, 3).reshape(slab, depth, cells)
 
 

time: 57.5 us -> 52.5 us (0.913)
  Pallas kernels: 55.5 us -> 51.6 us
  local copies, waits for them, and re-layouts: 1.87 us -> 0.8 us
    pallas_call x1, Pallas kernels: 55.5 us -> 51.6 us  [body(): pl.pallas_call(functools.partial(kernel, n_grid, n_lev), out_shape=jax.Sh...]
    unnamed x1, local copies, waits for them, and re-layouts: 1.87 us -> 0.8 us
where the time goes in v3:
time: 52.5 us; the launch traced here: 52.4 us
  Pallas kernels  51.6 us (98%)
  local copies, waits for them, and re-layouts  0.8 us (2%)
    pallas_call x1, Pallas kernels, body(): pl.pallas_call(functools.partial(kernel, n_grid, n_lev), out_shape=jax.Sh...  51.6 us

profile of v3, /device:TPU:1, one launch (start us, length us, event | category | flops | bytes accessed | tf_op | source)
XLA Modules:
  0.0 52.4 jit_solution(4280196891924458479)
XLA Ops:
  0.0 51.6 %shard_map.73 = f32[2,512,128]{2,1,0:T(8,128)S(1)} custom-call(s32[4]{0:T(128)} %owner_h.1, f32[2,4]{1,0:T(2,128)} %cw_h.1, f32[2,512,128]{2,1,0:T(8,128)} %bitcast.12, s32[4,4,64]{2,1,0:T(4,128)} %off_h.1, f32[4,1,64]{2,1,0:T(1,128)} %val_h.1, f32[4,1,64]{2,1,0:T(1,128)} %err_h.1, s32[4,1,128]{2,1,0:T(1,128)} %bitcast.13), custom_call_target="tpu_custom_call" | custom-call | tf_op jit(solution)/shard_map/pallas_call | solution.py:392
  51.6 0.8 %copy.11 = f32[2,2,32768]{2,1,0:T(2,128)} copy(f32[2,2,32768]{2,1,0:T(2,128)S(1)} %bitcast.11) | data formatting | bytes 1048576

commit v4 on v3

--- a/solution.py
+++ b/solution.py
@@ -42,7 +42,7 @@
 def kernel(
     n_grid, n_lev, owner_h, cw_h, x_h, off_h, val_h, err_h, anc_h, out,
     owner, cw, x, off, val, err, anc, pay, zbuf, first, picks, gath, f, y, ys, ssend, srecv, csend, crecv, tiles_s,
-    load_sem, z_sem, f_sem, p_sem, g_sem, in_sem, out_sem, s_sem, r_sem,
+    load_sem, z_sem, f_sem, p_sem, y_sem, g_sem, in_sem, out_sem, s_sem, r_sem,
 ):
     slab = x.shape[0]
     rows = x.shape[1] // n_grid
@@ -187,6 +187,20 @@
 
     drain(zbuf.at[pl.ds(0, n_z - 1)], z_sem.at[1])
     z2 = zbuf.reshape(n_z * 24, LANES)
+    def spread_rows(b):
+        for r in range(4):
+            tiles_s[BATCH_TILE + 4 * (b - 1) + r] = z2[pl.ds(BASE_ROW[b] + r, n_z, stride=24), :]
+        mine = tiles_s.at[pl.ds(BATCH_TILE + 4 * (b - 1), 4)]
+        for d in range(1, n_y):
+            send(mine, gath.at[b - 1, my_col], y_sem.at[b - 1], zz * n_col + ((yy + d) % n_y) * n_core + core, lev)
+        gath[b - 1, my_col] = tiles_s[BATCH_TILE + 4 * (b - 1) : BATCH_TILE + 4 * b]
+
+    def cross_rows(b):
+        drain(gath.at[b - 1, pl.ds(0, n_y - 1)], y_sem.at[b - 1, 1])
+        mine = gath.at[b - 1, pl.ds(core * n_y, n_y)]
+        send(mine, mine, g_sem.at[b - 1], me + 1 - 2 * core, lev)
+
+    spread_rows(1)
     for g in range(n_lev):
         a = z2[pl.ds((g // 2) * 2, n_z, stride=24), :]
         c = z2[pl.ds((g // 2) * 2 + 1, n_z, stride=24), :]
@@ -208,17 +222,11 @@
     for d in range(1, n_col):
         send(tiles_s.at[n_lev], picks.at[my_col], p_sem, col_peer(d), lev)
     picks[my_col] = tiles_s[n_lev]
-    for b in range(1, NB):
-        for r in range(4):
-            tiles_s[BATCH_TILE + 4 * (b - 1) + r] = z2[pl.ds(BASE_ROW[b] + r, n_z, stride=24), :]
-        mine = tiles_s.at[pl.ds(BATCH_TILE + 4 * (b - 1), 4)]
-        for d in range(1, n_col):
-            send(mine, gath.at[b - 1, my_col], g_sem.at[b - 1], col_peer(d), lev)
-        gath[b - 1, my_col] = tiles_s[BATCH_TILE + 4 * (b - 1) : BATCH_TILE + 4 * b]
+    spread_rows(2)
+    spread_rows(3)
 
     def push_in(t, carry):
-        far = (t + 1) // 2
-        peer = (me + far + (1 - t % 2) * (n_grid - 2 * far)) % n_grid
+        peer = (me + t * 27) % n_grid
         send(
             x.at[:, pl.ds(pl.multiple_of(peer * rows, rows), rows), :],
             f.at[pl.ds(my_slot * slab, slab)],
@@ -302,6 +310,8 @@
             row = row + crecv[b - 1, d]
         return prior + row[0:1, :]
 
+    for b in range(1, NB):
+        cross_rows(b)
     drain(first.at[pl.ds(0, n_lev * n_col - 1)], f_sem.at[1])
     prior = first[:n_col]
     for level in range(1, n_lev):
@@ -315,7 +325,7 @@
         chosen = chosen + picks[k]
     pair_cols = columns(chosen)
     for b in range(1, NB):
-        drain(gath.at[b - 1, pl.ds(0, n_col - 1)], g_sem.at[b - 1, 1])
+        drain(gath.at[b - 1, pl.ds(0, n_y)], g_sem.at[b - 1, 1])
         v = member_values(b)
         if b == 1:
             move(1, change[0][1], v)
@@ -338,16 +348,14 @@
         mean_row = mean_row + jnp.sum(change[b][0] * chain[b], axis=0, keepdims=True)
 
     total = chain[NB] + mean_row
-    t_hi, t_mid, t_low = split3(total)
+    t_hi, t_mid, _ = split3(total)
     drain(f.at[pl.ds(0, members - slab)], in_sem.at[1])
     f2 = f.reshape(members * rows, LANES)
     y2 = y.reshape(members * rows, LANES)
     for s in range(rows):
         two = [f2[pl.ds(i * rows + s, n_grid, stride=slab * rows), :] for i in range(slab)]
-        hi, mid, low = split3(jnp.concatenate(two, axis=0))
-        mixed = (dot(t_low, hi) + dot(t_mid, mid)) + dot(t_hi, low)
-        mixed = mixed + (dot(t_mid, hi) + dot(t_hi, mid))
-        mixed = mixed + dot(t_hi, hi)
+        hi, mid, _ = split3(jnp.concatenate(two, axis=0))
+        mixed = (dot(t_mid, hi) + dot(t_hi, mid)) + dot(t_hi, hi)
         for i in range(slab):
             y2[pl.ds(i * rows + s, n_grid, stride=slab * rows), :] = mixed[i * n_grid : (i + 1) * n_grid]
 
@@ -367,7 +375,8 @@
     drain(first.at[pl.ds(0, n_lev * n_col - 1)], f_sem.at[0])
     drain(picks.at[pl.ds(0, n_col - 1)], p_sem.at[0])
     for b in range(NB - 1):
-        drain(gath.at[b, pl.ds(0, n_col - 1)], g_sem.at[b, 0])
+        drain(gath.at[b, pl.ds(0, n_y - 1)], y_sem.at[b, 0])
+        drain(gath.at[b, pl.ds(0, n_y)], g_sem.at[b, 0])
     drain(f.at[pl.ds(0, members - slab)], in_sem.at[0])
     for b in range(NB - 1):
         drain(srecv.at[b], s_sem.at[b, 0])
@@ -418,6 +427,7 @@
             pltpu.SemaphoreType.DMA((7,)),
             pair, pair, pair,
             pltpu.SemaphoreType.DMA((NB - 1, 2)),
+            pltpu.SemaphoreType.DMA((NB - 1, 2)),
             pair, pair,
             pltpu.SemaphoreType.DMA((NB - 1, 2)),
             pltpu.SemaphoreType.DMA((NB - 1, 2)),

time: 52.5 us -> 49.8 us (0.949)
  Pallas kernels: 51.6 us -> 49 us
    pallas_call x1, Pallas kernels: 51.6 us -> 49 us  [body(): pl.pallas_call(functools.partial(kernel, n_grid, n_lev), out_shape=jax.Sh...]
where the time goes in v4:
time: 49.8 us
  Pallas kernels  49 us (98%)
  local copies, waits for them, and re-layouts  0.8 us (2%)
    pallas_call x1, Pallas kernels, body(): pl.pallas_call(functools.partial(kernel, n_grid, n_lev), out_shape=jax.Sh...  49 us

profile of v4, /device:TPU:1, one launch (start us, length us, event | category | flops | bytes accessed | tf_op | source)
XLA Modules:
  0.0 49.8 jit_solution(4793127701659390013)
XLA Ops:
  0.0 49.0 %shard_map.73 = f32[2,512,128]{2,1,0:T(8,128)S(1)} custom-call(s32[4]{0:T(128)} %owner_h.1, f32[2,4]{1,0:T(2,128)} %cw_h.1, f32[2,512,128]{2,1,0:T(8,128)} %bitcast.12, s32[4,4,64]{2,1,0:T(4,128)} %off_h.1, f32[4,1,64]{2,1,0:T(1,128)} %val_h.1, f32[4,1,64]{2,1,0:T(1,128)} %err_h.1, s32[4,1,128]{2,1,0:T(1,128)} %bitcast.13), custom_call_target="tpu_custom_call" | custom-call | tf_op jit(solution)/shard_map/pallas_call | solution.py:401
  49.0 0.8 %copy.11 = f32[2,2,32768]{2,1,0:T(2,128)} copy(f32[2,2,32768]{2,1,0:T(2,128)S(1)} %bitcast.11) | data formatting | bytes 1048576

commit v5 on v4

--- a/solution.py
+++ b/solution.py
@@ -201,6 +201,16 @@
         send(mine, mine, g_sem.at[b - 1], me + 1 - 2 * core, lev)
 
     spread_rows(1)
+    z_of_row = iota((n_z, LANES), 0)
+    rows_of = [z2[pl.ds(4 + i, n_z, stride=24), :] for i in range(NB - 1)]
+    found = [
+        jnp.sum(jnp.where(z_of_row * n_col + yy * n_core + core == owner[b], rows_of[i], 0.0), axis=0, keepdims=True)
+        for b, i in PAIRS
+    ]
+    tiles_s[n_lev] = jnp.concatenate(found + found[:2], axis=0)
+    for d in range(1, n_col):
+        send(tiles_s.at[n_lev], picks.at[my_col], p_sem, col_peer(d), lev)
+    picks[my_col] = tiles_s[n_lev]
     for g in range(n_lev):
         a = z2[pl.ds((g // 2) * 2, n_z, stride=24), :]
         c = z2[pl.ds((g // 2) * 2 + 1, n_z, stride=24), :]
@@ -212,16 +222,6 @@
                 send(tiles_s.at[level], first.at[lev * n_col + my_col], f_sem, col_peer(d), level)
     first[lev * n_col + my_col] = tiles_s[lev]
 
-    z_of_row = iota((n_z, LANES), 0)
-    rows_of = [z2[pl.ds(4 + i, n_z, stride=24), :] for i in range(NB - 1)]
-    found = [
-        jnp.sum(jnp.where(z_of_row * n_col + yy * n_core + core == owner[b], rows_of[i], 0.0), axis=0, keepdims=True)
-        for b, i in PAIRS
-    ]
-    tiles_s[n_lev] = jnp.concatenate(found + found[:2], axis=0)
-    for d in range(1, n_col):
-        send(tiles_s.at[n_lev], picks.at[my_col], p_sem, col_peer(d), lev)
-    picks[my_col] = tiles_s[n_lev]
     spread_rows(2)
     spread_rows(3)
 
@@ -328,8 +328,8 @@
         drain(gath.at[b - 1, pl.ds(0, n_y)], g_sem.at[b - 1, 1])
         v = member_values(b)
         if b == 1:
+            base(1, v, pair_cols)
             move(1, change[0][1], v)
-            base(1, v, pair_cols)
             push_shift(1)
             push_blocks(2)
         else:

time: 49.8 us -> 49.9 us (level)
  no operation moved by 1% of the time
where the time goes in v5:
time: 49.9 us; the launch traced here: 49.8 us
  Pallas kernels  49 us (98%)
  local copies, waits for them, and re-layouts  0.8 us (2%)
    pallas_call x1, Pallas kernels, body(): pl.pallas_call(functools.partial(kernel, n_grid, n_lev), out_shape=jax.Sh...  49 us

profile of v5, /device:TPU:1, one launch (start us, length us, event | category | flops | bytes accessed | tf_op | source)
XLA Modules:
  0.0 49.8 jit_solution(3303472813877382006)
XLA Ops:
  0.0 49.0 %shard_map.73 = f32[2,512,128]{2,1,0:T(8,128)S(1)} custom-call(s32[4]{0:T(128)} %owner_h.1, f32[2,4]{1,0:T(2,128)} %cw_h.1, f32[2,512,128]{2,1,0:T(8,128)} %bitcast.12, s32[4,4,64]{2,1,0:T(4,128)} %off_h.1, f32[4,1,64]{2,1,0:T(1,128)} %val_h.1, f32[4,1,64]{2,1,0:T(1,128)} %err_h.1, s32[4,1,128]{2,1,0:T(1,128)} %bitcast.13), custom_call_target="tpu_custom_call" | custom-call | tf_op jit(solution)/shard_map/pallas_call | solution.py:401
  49.0 0.8 %copy.11 = f32[2,2,32768]{2,1,0:T(2,128)} copy(f32[2,2,32768]{2,1,0:T(2,128)S(1)} %bitcast.11) | data formatting | bytes 1048576
